TPU v7x, 32 devices: a whole 2x2x4 slice. The times are simulated.
32 devices in a mesh: mem: 8 (over z, y), job: 4 (over x, core).
Axes of the slice: x: 2, y: 2, z: 4, core: 2. Of those that a mesh axis runs over, the one named last changes fastest.
Arguments:
- pair_cost: bfloat16 [1536, 128, 128], P(('mem', 'job')), may hold values from -6 to 6
- pair_coef: bfloat16 [1536, 128, 128], P(('mem', 'job')), may hold values from 0.049804688 to 0.5
- slot_member: int32 [32, 48], P(('mem', 'job')), may hold values from 0 to 31, never falling along the last dimension, each value on 1 to 4 neighbouring positions
- slot_owner: int32 [32, 48, 1], P(('mem', 'job')), may hold values from 0 to 7; in each aligned block of 48 rows (0 to 47, 48 to 95, ..., all dimensions but the last counted through in order) at most 9 rows name the same one
- slot_local: int32 [32, 48], P(('mem', 'job')), may hold values from 0 to 15
- duals: float32 [512, 128], P(('mem', 'job')), may hold values from 0.1 to 3
- capacity: int32 [512, 128], P(('mem', 'job')), may hold values from 0 to 39
Outputs:
- primal: bfloat16 [1536, 128, 128], P(('mem', 'job'))
- gradient: float32 [512, 128], P(('mem', 'job'))
- member_share: float32 [256, 128], P('mem')
Inputs may be any that keep to these rules, and one draw needn't show every extreme that they name: `slot_member`: in each device's row the values never fall, every value appears, none more than 4 times, and one exactly 4 times. `slot_owner`: among the 48 entries of one device no value appears more than 9 times, and in some devices one appears exactly 9 times.
All inputs are finite; a program needn't handle non-finite values.
Results may differ from a plain program's by a relative error of at most 0.001.
Values sent between devices are 32-bit elements; how exact they have to be, the bound alone decides.
A program may use at most 64 MiB of HBM per device.

v0:
```python
import jax
import jax.numpy as jnp
from jax import lax
from jax.sharding import PartitionSpec as P

MB_DEV = 32


RIDGE = 1.0


def allocate(pair_cost, pair_coef, dual_rows):
    reduced = pair_cost.astype(jnp.float32) + pair_coef.astype(jnp.float32) * dual_rows[:, None, :]
    allocation = jnp.clip(-reduced / RIDGE, 0.0, 1.0)
    column_part = jnp.sum(pair_coef.astype(jnp.float32) * allocation, axis=1)
    row_part = jnp.sum(allocation, axis=2)
    return (allocation.astype(jnp.bfloat16), column_part, row_part)


def per_device(pair_cost, pair_coef, slot_member, slot_owner, slot_local, duals, capacity):
    slot_count = pair_cost.shape[0]
    block_size = pair_cost.shape[1]
    job_blocks = duals.shape[0]
    mem_count = lax.axis_size("mem")
    owner_index = slot_owner[0, :, 0]
    local_index = slot_local[0]
    peer_slots = max(2, (3 * slot_count + 2 * mem_count - 1) // (2 * mem_count))
    owner_table = (owner_index[:, None] == jnp.arange(mem_count, dtype=jnp.int32)[None, :]).astype(
        jnp.int32
    )
    slot_rank = jnp.sum((jnp.cumsum(owner_table, axis=0) - owner_table) * owner_table, axis=1)
    position = owner_index * peer_slots + slot_rank
    requests = jnp.zeros((mem_count * peer_slots,), jnp.int32).at[position].set(local_index)
    requests = requests.reshape(mem_count, peer_slots)
    received = lax.all_to_all(requests, "mem", split_axis=0, concat_axis=0, tiled=True)
    replies = duals[received]
    fetched, received = (
        lax.all_to_all(replies, "mem", split_axis=0, concat_axis=0, tiled=True),
        received,
    )
    dual_rows = fetched.reshape(mem_count * peer_slots, block_size)[position]
    primal, column_part, row_part = allocate(pair_cost, pair_coef, dual_rows)
    outgoing = (
        jnp.zeros((mem_count * peer_slots, block_size), jnp.float32).at[position].set(column_part)
    )
    incoming = lax.all_to_all(
        outgoing.reshape(mem_count, peer_slots, block_size),
        "mem",
        split_axis=0,
        concat_axis=0,
        tiled=True,
    )
    totals = jax.ops.segment_sum(
        incoming.reshape(mem_count * peer_slots, block_size),
        received.reshape(-1),
        num_segments=job_blocks,
    )
    gradient = totals - capacity.astype(jnp.float32)
    member_table = (jnp.arange(MB_DEV, dtype=jnp.int32)[:, None] == slot_member[0][None, :]).astype(
        jnp.float32
    )
    member_part = jnp.dot(
        member_table, row_part, precision=lax.Precision.HIGHEST, preferred_element_type=jnp.float32
    )
    member_share = lax.psum(member_part, "job") / block_size
    return (primal, gradient, member_share)


def solution(mesh):
    placed = (
        P(("mem", "job"), None, None),
        P(("mem", "job"), None, None),
        P(("mem", "job"), None),
        P(("mem", "job"), None, None),
        P(("mem", "job"), None),
        P(("mem", "job"), None),
        P(("mem", "job"), None),
    )
    return jax.shard_map(
        per_device,
        mesh=mesh,
        in_specs=placed,
        out_specs=(P(("mem", "job"), None, None), P(("mem", "job"), None), P("mem", None)),
        check_vma=False,
    )
```

profile of v0, /device:TPU:0, one launch (start us, length us, event | category | flops | bytes accessed | tf_op | source)
XLA Modules:
  0.0 57.0 jit_solution(11159333356886695551)
XLA Ops:
  0.6 0.0 copy-start
  0.6 0.7 %fusion.6 = s32[48,8]{1,0:T(8,128)S(1)} fusion(s32[48]{0:T(128)} %bitcast.20), kind=kLoop, calls=%fused_computation.15 | loop fusion | flops 768 | bytes 1728 | tf_op jit(solution)/shard_map/convert_element_type | solution.py:28
  1.4 0.1 reduce_window_sum.11
  1.5 0.8 %select_reduce_fusion = s32[48]{0:T(128)S(1)} fusion(s32[48,8]{1,0:T(8,128)S(1)} %reduce_window_sum.11, s32[48]{0:T(128)} %bitcast.21), kind=kLoop, calls=%fused_computation.13 | loop fusion | flops 1872 | bytes 1920 | tf_op jit(solution)/shard_map/reduce_sum | solution.py:31
  2.3 0.7 %fusion.13 = s32[48]{0:T(128)S(1)} fusion(s32[48]{0:T(128)S(1)} %select_reduce_fusion, s32[1,48,1]{1,2,0:T(1,128)} %param.10), kind=kLoop, calls=%fused_computation.29 | loop fusion | flops 240 | bytes 576 | tf_op jit(solution)/shard_map/select_n | solution.py:33
  3.0 0.9 %scatter_custom_fusion = s32[72]{0:T(128)S(1)} fusion(s32[48]{0:T(128)S(1)} %fusion.13, s32[48]{0:T(128)} %bitcast.23, s32[]{:T(128)} %constant.8.clone.1), kind=kCustom, calls=%fused_computation.31 | custom fusion | bytes 800 | tf_op jit(solution)/shard_map/scatter | solution.py:33
  3.8 0.1 all_to_all.14
  3.9 13.6 %all_to_all.22 = s32[8,1,9]{2,1,0:T(1,128)S(1)} all-to-all(s32[8,1,9]{2,1,0:T(1,128)S(1)} %bitcast.19), channel_id=1, replica_groups=mesh['mem'=8,'job'=4] {'mem'}, dimensions={0} | all-to-all | bytes 576 | tf_op jit(solution)/shard_map/all_to_all | solution.py:35
  17.5 0.1 reshape.83
  17.6 0.0 copy-done
  17.6 0.6 %gather_fusion = f32[72,128]{1,0:T(8,128)S(1)} fusion(f32[16,128]{1,0:T(8,128)S(1)} %copy-done, s32[1024]{0:T(1024)S(1)} %pad_clamp_fusion.1), kind=kCustom, calls=%fused_computation | custom fusion | bytes 74016 | tf_op jit(solution)/shard_map/gather | solution.py:36
  18.2 0.6 %reshape.82 = f32[8,9,128]{2,1,0:T(8,128)} reshape(f32[72,128]{1,0:T(8,128)S(1)} %gather_fusion) | data formatting | bytes 73728 | tf_op jit(solution)/shard_map/gather | solution.py:36
  18.8 3.4 %all-to-all-start.1 = ((f32[8,9,128]{2,1,0:T(8,128)}), f32[8,9,128]{2,1,0:T(8,128)S(1)}, u32[]{:S(2)}, u32[]{:S(2)}) async-start(f32[8,9,128]{2,1,0:T(8,128)} %reshape.82), calls=%async_computation.1 | async-start | bytes 131072 | tf_op jit(solution)/shard_map/all_to_all | solution.py:38
  22.2 0.5 broadcast.65
  22.7 0.7 %reduce.3 = s32[8,9]{1,0:T(8,128)S(1)} reduce(s32[8,1,9]{2,1,0:T(1,128)S(1)} %all_to_all.22, s32[]{:T(128)} %broadcast.65), dimensions={1}, to_apply=%all_to_all.15.reduce_sub_computation.3 | reduce | bytes 580 | tf_op jit(solution)/shard_map/all_to_all | solution.py:35
  23.4 0.1 reshape.115
  23.5 5.6 %all-to-all-done.1 = f32[8,9,128]{2,1,0:T(8,128)S(1)} async-done(((f32[8,9,128]{2,1,0:T(8,128)}), f32[8,9,128]{2,1,0:T(8,128)S(1)}, u32[]{:S(2)}, u32[]{:S(2)}) %all-to-all-start.1) | async-done | bytes 36896 | tf_op jit(solution)/shard_map/all_to_all | solution.py:38
  29.0 0.6 %gather_fusion.1 = f32[48,128]{1,0:T(8,128)S(1)} fusion(f32[72,128]{1,0:T(8,128)S(1)} %reshape.78, s32[1024]{0:T(1024)S(1)} %pad_clamp_fusion), kind=kCustom, calls=%fused_computation.1 | custom fusion | bytes 49344 | tf_op jit(solution)/shard_map/gather | solution.py:41
  29.6 0.0 copy-start.2
  29.6 0.0 copy-start.1
  29.6 4.1 %fusion.4 = (f32[48,128]{1,0:T(8,128)S(1)}, f32[48,128]{1,0:T(8,128)S(1)}, bf16[48,128,128]{2,1,0:T(8,128)(2,1)}) fusion(bf16[48,128,128]{2,1,0:T(8,128)(2,1)} %param.8, bf16[48,128,128]{2,1,0:T(8,128)(2,1)} %param.7, f32[48,128]{1,0:T(8,128)S(1)} %gather_fusion.1), kind=kLoop, calls=%fused_computation.11 | loop fusion | flops 7852032 | bytes 4792320 | tf_op jit(solution)/shard_map/reduce_sum | solution.py:16
  33.8 0.0 copy-done.2
  33.8 0.1 fusion.9
  33.9 10.1 %psum.7 = f32[32,128]{1,0:T(8,128)S(1)} all-reduce(f32[32,128]{1,0:T(8,128)S(1)} %fusion.9), channel_id=1, replica_groups=mesh['mem'=8,'job'=4] {'job'}, use_global_device_ids=true, to_apply=%region_7.8 | all-reduce | flops 4096 | bytes 32768 | tf_op jit(solution)/shard_map/psum | solution.py:65
  44.0 0.7 %scatter_custom_fusion.1 = f32[72,128]{1,0:T(8,128)S(1)} fusion(s32[48]{0:T(128)S(1)} %fusion.13, f32[48,128]{1,0:T(8,128)S(1)} %get-tuple-element.4, f32[]{:T(128)} %constant.7.clone.1), kind=kCustom, calls=%fused_computation.16 | custom fusion | bytes 36868 | tf_op jit(solution)/shard_map/scatter | solution.py:44
  44.7 0.6 %reshape.79 = f32[8,9,128]{2,1,0:T(8,128)} reshape(f32[72,128]{1,0:T(8,128)S(1)} %scatter_custom_fusion.1) | data formatting | bytes 73728 | tf_op jit(solution)/shard_map/reshape | solution.py:47
  45.3 3.3 %all-to-all-start.2 = ((f32[8,9,128]{2,1,0:T(8,128)}), f32[8,9,128]{2,1,0:T(8,128)S(1)}, u32[]{:S(2)}, u32[]{:S(2)}) async-start(f32[8,9,128]{2,1,0:T(8,128)} %reshape.79), calls=%async_computation.2 | async-start | bytes 131072 | tf_op jit(solution)/shard_map/all_to_all | solution.py:46
  48.7 0.6 %broadcast_multiply_fusion = f32[32,128]{1,0:T(8,128)} fusion(f32[32,128]{1,0:T(8,128)S(1)} %psum.7), kind=kLoop, calls=%fused_computation.21 | loop fusion | flops 4096 | bytes 32768 | tf_op jit(solution)/shard_map/div | solution.py:65
  49.3 6.2 %all-to-all-done.2 = f32[8,9,128]{2,1,0:T(8,128)S(1)} async-done(((f32[8,9,128]{2,1,0:T(8,128)}), f32[8,9,128]{2,1,0:T(8,128)S(1)}, u32[]{:S(2)}, u32[]{:S(2)}) %all-to-all-start.2) | async-done | bytes 36896 | tf_op jit(solution)/shard_map/all_to_all | solution.py:46
  55.5 0.9 %scatter_custom_fusion.2 = f32[16,128]{1,0:T(8,128)S(1)} fusion(s32[72]{0:T(128)S(1)} %reshape.115, f32[72,128]{1,0:T(8,128)S(1)} %reshape.117, f32[]{:T(128)} %constant.7.clone.1), kind=kCustom, calls=%fused_computation.26 | custom fusion | flops 9216 | bytes 8196 | tf_op jit(solution)/shard_map/scatter-add | solution.py:53
  56.4 0.0 copy-done.1
  56.4 0.6 %convert_subtract_fusion = f32[16,128]{1,0:T(8,128)} fusion(f32[16,128]{1,0:T(8,128)S(1)} %scatter_custom_fusion.2, s32[16,128]{1,0:T(8,128)S(1)} %copy-done.1), kind=kLoop, calls=%fused_computation.23 | loop fusion | flops 4096 | bytes 24576 | tf_op jit(solution)/shard_map/sub | solution.py:58
  (5 shorter events, 0.0 us)
Async XLA Ops:
  0.6 17.0 %copy-start = (f32[16,128]{1,0:T(8,128)S(1)}, f32[16,128]{1,0:T(8,128)}, u32[]{:S(2)}) copy-start(f32[16,128]{1,0:T(8,128)} %param.12) | copy-start | bytes 24580
  18.8 10.2 %all-to-all-start.1 = ((f32[8,9,128]{2,1,0:T(8,128)}), f32[8,9,128]{2,1,0:T(8,128)S(1)}, u32[]{:S(2)}, u32[]{:S(2)}) async-start(f32[8,9,128]{2,1,0:T(8,128)} %reshape.82), calls=%async_computation.1 | async-start | bytes 131072 | tf_op jit(solution)/shard_map/all_to_all | solution.py:38
  29.6 4.1 %copy-start.2 = (s32[1,48]{1,0:T(1,128)S(1)}, s32[1,48]{1,0:T(1,128)}, u32[]{:S(2)}) copy-start(s32[1,48]{1,0:T(1,128)} %param.9) | copy-start | bytes 580
  29.6 26.7 %copy-start.1 = (s32[16,128]{1,0:T(8,128)S(1)}, s32[16,128]{1,0:T(8,128)}, u32[]{:S(2)}) copy-start(s32[16,128]{1,0:T(8,128)} %param.13) | copy-start | bytes 24580
  45.3 10.2 %all-to-all-start.2 = ((f32[8,9,128]{2,1,0:T(8,128)}), f32[8,9,128]{2,1,0:T(8,128)S(1)}, u32[]{:S(2)}, u32[]{:S(2)}) async-start(f32[8,9,128]{2,1,0:T(8,128)} %reshape.79), calls=%async_computation.2 | async-start | bytes 131072 | tf_op jit(solution)/shard_map/all_to_all | solution.py:46
where the time goes:
time: 57.4 us; the launch traced here: 57 us
  blocking collectives  23.7 us (41%)
  waiting for transfers between devices  11.8 us (21%)
  other arithmetic  9.16 us (16%)
  starting transfers between devices  6.7 us (12%)
  local copies, waits for them, and re-layouts  4.76 us (8%)
  between operations  0.73 us (1%)
    all_to_all x1, blocking collectives, per_device(): lax.all_to_all(requests, 'mem', split_axis=0, concat_axis=0, tiled=True)  13.6 us
    psum x1, blocking collectives, per_device(): member_share = lax.psum(member_part, 'job') / block_size  10.1 us
    all_to_all x1, waiting for transfers between devices, per_device(): lax.all_to_all(outgoing.reshape(mem_count, peer_slots, block_size), 'mem'...  6.23 us
    all_to_all x1, waiting for transfers between devices, per_device(): lax.all_to_all(replies, 'mem', split_axis=0, concat_axis=0, tiled=True)  5.57 us
    reduce_sum x1, other arithmetic, allocate(): row_part = jnp.sum(allocation, axis=2)  4.11 us
    all_to_all x1, starting transfers between devices, per_device(): lax.all_to_all(replies, 'mem', split_axis=0, concat_axis=0, tiled=True)  3.35 us
    all_to_all x1, starting transfers between devices, per_device(): lax.all_to_all(outgoing.reshape(mem_count, peer_slots, block_size), 'mem'...  3.35 us
    gather x2, local copies, waits for them, and re-layouts, per_device(): replies = duals[received]  1.24 us
  transfers between devices with their start and end apart: 2, of which 2 were waited for; matrix products, arithmetic and copies ran while one was open for 3% of the time, Pallas kernels for 0%

commit v1 on v0

v1 whole, which is shorter than its diff:
```python
import functools

import jax
import jax.numpy as jnp
from jax import lax
from jax.experimental import pallas as pl
from jax.experimental.pallas import tpu as pltpu
from jax.sharding import PartitionSpec as P

MB_DEV = 32
CHUNK = 8

MESH = pl.DeviceIdType.MESH


def kernel(
    mem_count,
    job_count,
    cost_ref,
    coef_ref,
    member_ref,
    owner_ref,
    local_ref,
    duals_ref,
    capacity_ref,
    primal_ref,
    gradient_ref,
    share_ref,
    cost_v,
    coef_v,
    primal_v,
    member_s,
    owner_s,
    local_s,
    owner_v,
    local_v,
    capacity_v,
    table,
    column,
    totals,
    incoming,
    member_part,
    member_in,
    load_sem,
    small_sem,
    store_sem,
    gather_send,
    gather_recv,
    column_send,
    column_recv,
    member_send,
    member_recv,
):
    slots, block = cost_v.shape[0], cost_v.shape[1]
    jobs = duals_ref.shape[0]
    chunk = min(CHUNK, slots)
    chunks = slots // chunk
    my_mem = lax.axis_index("mem")
    my_job = lax.axis_index("job")

    barrier = pltpu.get_barrier_semaphore()

    def mem_peer(step):
        return lax.rem(my_mem + step, mem_count)

    def job_peer(step):
        return lax.rem(my_job + step, job_count)

    for step in range(1, mem_count):
        pl.semaphore_signal(
            barrier, inc=1, device_id=(mem_peer(step), my_job), device_id_type=MESH
        )
    for step in range(1, job_count):
        pl.semaphore_signal(
            barrier, inc=1, device_id=(my_mem, job_peer(step)), device_id_type=MESH
        )

    own_rows = pl.ds(pl.multiple_of(my_mem * jobs, jobs), jobs)
    small = [
        pltpu.make_async_copy(duals_ref, table.at[own_rows], small_sem.at[0]),
        pltpu.make_async_copy(owner_ref, owner_s, small_sem.at[1]),
        pltpu.make_async_copy(local_ref, local_s, small_sem.at[2]),
        pltpu.make_async_copy(member_ref, member_s, small_sem.at[3]),
        pltpu.make_async_copy(owner_ref, owner_v, small_sem.at[4]),
        pltpu.make_async_copy(local_ref, local_v, small_sem.at[5]),
        pltpu.make_async_copy(capacity_ref, capacity_v, small_sem.at[6]),
    ]
    for copy in small:
        copy.start()
    loads = []
    for part in range(chunks):
        rows = pl.ds(part * chunk, chunk)
        for index, (source, target) in enumerate(((cost_ref, cost_v), (coef_ref, coef_v))):
            copy = pltpu.make_async_copy(
                source.at[rows], target.at[rows], load_sem.at[2 * part + index]
            )
            copy.start()
            loads.append(copy)
    small[0].wait()

    pl.semaphore_wait(barrier, mem_count + job_count - 2)

    gathers = []
    for step in range(1, mem_count):
        copy = pltpu.make_async_remote_copy(
            src_ref=table.at[own_rows],
            dst_ref=table.at[own_rows],
            send_sem=gather_send.at[step - 1],
            recv_sem=gather_recv.at[step - 1],
            device_id=(mem_peer(step), my_job),
            device_id_type=MESH,
        )
        copy.start()
        gathers.append(copy)
    for copy in small[1:]:
        copy.wait()
    for copy in loads:
        copy.wait()
    for copy in gathers:
        copy.wait_recv()

    lanes = lax.broadcasted_iota(jnp.int32, (block, block), 1)
    stores = []
    members = jnp.zeros((block, block), jnp.float32)
    for part in range(chunks):

        def pair(index, members, part=part):
            halves = []
            marks = []
            for side in range(2):
                slot = part * chunk + 2 * index + side
                row = owner_s[0, slot] * jobs + local_s[0, slot]
                dual = -table[pl.ds(row, 1), :]
                coef = coef_v[slot].astype(jnp.float32)
                allocation = jnp.clip(
                    coef * dual - cost_v[slot].astype(jnp.float32), 0.0, 1.0
                )
                primal = allocation.astype(jnp.bfloat16)
                primal_v[slot] = primal
                column[pl.ds(slot, 1), :] = jnp.sum(coef * allocation, axis=0, keepdims=True)
                halves.append(primal)
                marks.append((lanes == member_s[0, slot]).astype(jnp.float32).astype(jnp.bfloat16))
            return members + jnp.dot(
                jnp.concatenate(halves, axis=1),
                jnp.concatenate(marks, axis=0),
                preferred_element_type=jnp.float32,
            )

        members = lax.fori_loop(0, chunk // 2, pair, members, unroll=2)
        rows = pl.ds(part * chunk, chunk)
        copy = pltpu.make_async_copy(primal_v.at[rows], primal_ref.at[rows], store_sem.at[part])
        copy.start()
        stores.append(copy)

    named = owner_v[...] * jobs + local_v[...]
    match = lax.broadcasted_iota(jnp.int32, (mem_count * jobs, slots), 0) == named
    match = match.astype(jnp.float32).astype(jnp.bfloat16)
    sums = column[...]
    high = sums.astype(jnp.bfloat16)
    low = (sums - high.astype(jnp.float32)).astype(jnp.bfloat16)
    totals[...] = jnp.dot(match, high, preferred_element_type=jnp.float32) + jnp.dot(
        match, low, preferred_element_type=jnp.float32
    )
    member_part[...] = members.T[:MB_DEV]

    sends = []
    for step in range(1, mem_count):
        peer = mem_peer(step)
        copy = pltpu.make_async_remote_copy(
            src_ref=totals.at[pl.ds(pl.multiple_of(peer * jobs, jobs), jobs)],
            dst_ref=incoming.at[step - 1],
            send_sem=column_send.at[step - 1],
            recv_sem=column_recv.at[step - 1],
            device_id=(peer, my_job),
            device_id_type=MESH,
        )
        copy.start()
        sends.append(copy)
    shares = []
    for step in range(1, job_count):
        copy = pltpu.make_async_remote_copy(
            src_ref=member_part,
            dst_ref=member_in.at[step - 1],
            send_sem=member_send.at[step - 1],
            recv_sem=member_recv.at[step - 1],
            device_id=(my_mem, job_peer(step)),
            device_id_type=MESH,
        )
        copy.start()
        shares.append(copy)

    share = member_part[...]
    for step, copy in enumerate(shares):
        copy.wait_recv()
        share = share + member_in[step]
    share_ref[...] = share * (1.0 / block)

    gradient = totals[own_rows, :] - capacity_v[...].astype(jnp.float32)
    for step, copy in enumerate(sends):
        copy.wait_recv()
        gradient = gradient + incoming[step]
    gradient_ref[...] = gradient

    for copy in gathers + sends + shares:
        copy.wait_send()
    for copy in stores:
        copy.wait()


def solution(mesh):
    mem_count, job_count = mesh.shape["mem"], mesh.shape["job"]
    row = P(("mem", "job"))

    def per_device(pair_cost, pair_coef, slot_member, slot_owner, slot_local, duals, capacity):
        slots, block, _ = pair_cost.shape
        jobs = duals.shape[0]
        chunks = slots // min(CHUNK, slots)
        anywhere = pl.BlockSpec(memory_space=pl.ANY)
        dma = pltpu.SemaphoreType.DMA
        return pl.pallas_call(
            functools.partial(kernel, mem_count, job_count),
            out_shape=(
                jax.ShapeDtypeStruct(pair_cost.shape, jnp.bfloat16),
                jax.ShapeDtypeStruct((jobs, block), jnp.float32),
                jax.ShapeDtypeStruct((MB_DEV, block), jnp.float32),
            ),
            in_specs=[anywhere] * 7,
            out_specs=(
                anywhere,
                pl.BlockSpec(memory_space=pltpu.VMEM),
                pl.BlockSpec(memory_space=pltpu.VMEM),
            ),
            scratch_shapes=[
                pltpu.VMEM(pair_cost.shape, jnp.bfloat16),
                pltpu.VMEM(pair_cost.shape, jnp.bfloat16),
                pltpu.VMEM(pair_cost.shape, jnp.bfloat16),
                pltpu.SMEM((1, slots), jnp.int32),
                pltpu.SMEM((1, slots), jnp.int32),
                pltpu.SMEM((1, slots), jnp.int32),
                pltpu.VMEM((1, slots), jnp.int32),
                pltpu.VMEM((1, slots), jnp.int32),
                pltpu.VMEM((jobs, block), jnp.int32),
                pltpu.VMEM((mem_count * jobs, block), jnp.float32),
                pltpu.VMEM((slots, block), jnp.float32),
                pltpu.VMEM((mem_count * jobs, block), jnp.float32),
                pltpu.VMEM((mem_count - 1, jobs, block), jnp.float32),
                pltpu.VMEM((MB_DEV, block), jnp.float32),
                pltpu.VMEM((job_count - 1, MB_DEV, block), jnp.float32),
                dma((2 * chunks,)),
                dma((7,)),
                dma((chunks,)),
                dma((mem_count - 1,)),
                dma((mem_count - 1,)),
                dma((mem_count - 1,)),
                dma((mem_count - 1,)),
                dma((job_count - 1,)),
                dma((job_count - 1,)),
            ],
            compiler_params=pltpu.CompilerParams(collective_id=0, has_side_effects=True),
        )(
            pair_cost,
            pair_coef,
            slot_member,
            slot_owner.reshape(1, slots),
            slot_local,
            duals,
            capacity,
        )

    return jax.shard_map(
        per_device,
        mesh=mesh,
        in_specs=(row,) * 7,
        out_specs=(row, row, P("mem")),
        check_vma=False,
    )
```

time: 57.4 us -> 23 us (0.40)
  blocking collectives: 23.7 us -> 0 us
  Pallas kernels: 0 us -> 18.2 us
  waiting for transfers between devices: 11.8 us -> 0 us
  other arithmetic: 9.16 us -> 0 us
  starting transfers between devices: 6.7 us -> 0 us
  local copies, waits for them, and re-layouts: 4.76 us -> 3.95 us
    pallas_call x0 -> x1, Pallas kernels: none -> 18.2 us  [per_device(): pl.pallas_call(functools.partial(kernel, mem_count, job_count), out_shape...]
    all_to_all x1 -> x0, blocking collectives: 13.6 us -> none  [per_device(): lax.all_to_all(requests, 'mem', split_axis=0, concat_axis=0, tiled=True)]
    all_to_all x2 -> x0, waiting for transfers between devices: 11.8 us -> none  [the longest x1 6.23 us: per_device(): lax.all_to_all(outgoing.reshape(mem_count, peer_slots, block_size), 'mem'...]
    psum x1 -> x0, blocking collectives: 10.1 us -> none  [per_device(): member_share = lax.psum(member_part, 'job') / block_size]
    all_to_all x2 -> x0, starting transfers between devices: 6.7 us -> none  [the longest x1 3.35 us: per_device(): lax.all_to_all(replies, 'mem', split_axis=0, concat_axis=0, tiled=True)]
    reduce_sum x2 -> x0, other arithmetic: 4.94 us -> none  [the longest x1 4.11 us: allocate(): row_part = jnp.sum(allocation, axis=2)]
    unnamed x6 -> x7, local copies, waits for them, and re-layouts: 0.02 us -> 3.95 us
    gather x3 -> x0, local copies, waits for them, and re-layouts: 1.82 us -> none  [the longest x2 1.24 us: per_device(): replies = duals[received]]
  transfers between devices with their start and end apart: 2 -> 0, of which waited for: 2 -> 0; matrix products, arithmetic and copies ran while one was open for 3% -> 0% of each run, Pallas kernels for 0% -> 0%
where the time goes in v1:
time: 23 us; the launch traced here: 22.8 us
  Pallas kernels  18.2 us (79%)
  local copies, waits for them, and re-layouts  3.95 us (17%)
  between operations  0.66 us (3%)
    pallas_call x1, Pallas kernels, per_device(): pl.pallas_call(functools.partial(kernel, mem_count, job_count), out_shape...  18.2 us
    unnamed x7, local copies, waits for them, and re-layouts  3.95 us

profile of v1, /device:TPU:0, one launch (start us, length us, event | category | flops | bytes accessed | tf_op | source)
XLA Modules:
  0.0 22.8 jit_solution(969020265747988276)
XLA Ops:
  0.6 18.2 %shard_map.94 = (bf16[48,128,128]{2,1,0:T(8,128)(2,1)}, f32[16,128]{1,0:T(8,128)}, f32[32,128]{1,0:T(8,128)}) custom-call(bf16[48,128,128]{2,1,0:T(8,128)(2,1)} %cost_ref.1, bf16[48,128,128]{2,1,0:T(8,128)(2,1)} %coef_ref.1, s32[1,48]{1,0:T(1,128)} %member_ref.1, s32[1,48]{1,0:T(1,128)} %bitcast.1, s32[1,48]{1,0:T(1,128)} %local_ref.1, f32[16,128]{1,0:T(8,128)} %duals_ref.1, ...), custom_call_target="tpu_custom_call" | custom-call | tf_op jit(solution)/shard_map/pallas_call | solution.py:220
  18.9 0.0 copy-start.1
  18.9 0.0 copy-start
  18.9 2.7 %copy.13 = bf16[48,128,128]{2,1,0:T(8,128)(2,1)} copy(bf16[48,128,128]{2,1,0:T(8,128)(2,1)} %get-tuple-element.6) | data formatting | bytes 3145728
  21.6 0.0 copy-done.1
  21.6 0.6 %copy.14 = f32[16,128]{1,0:T(8,128)} copy(f32[16,128]{1,0:T(8,128)S(1)} %copy-done.1) | data formatting | bytes 16384
  22.2 0.0 copy-done
  22.2 0.6 %copy.15 = f32[32,128]{1,0:T(8,128)} copy(f32[32,128]{1,0:T(8,128)S(1)} %copy-done) | data formatting | bytes 32768
Async XLA Ops:
  18.9 2.8 %copy-start.1 = (f32[16,128]{1,0:T(8,128)S(1)}, f32[16,128]{1,0:T(8,128)}, u32[]{:S(2)}) copy-start(f32[16,128]{1,0:T(8,128)} %get-tuple-element.7) | copy-start | bytes 24580
  18.9 3.4 %copy-start = (f32[32,128]{1,0:T(8,128)S(1)}, f32[32,128]{1,0:T(8,128)}, u32[]{:S(2)}) copy-start(f32[32,128]{1,0:T(8,128)} %get-tuple-element.8) | copy-start | bytes 49156

commit v2 on v1

--- a/solution.py
+++ b/solution.py
@@ -9,8 +9,31 @@
 
 MB_DEV = 32
 CHUNK = 8
+VMEM_LIMIT = 16 << 20
 
 MESH = pl.DeviceIdType.MESH
+
+
+def partner(index, distance, count):
+    assert count & (count - 1) == 0
+    bit = 1
+    while bit < count:
+        if distance & bit:
+            index = index + bit - 2 * bit * ((index // bit) % 2)
+        bit *= 2
+    return index
+
+
+def finish(primal_in, gradient_in, share_in, primal_ref, gradient_ref, share_ref, sem):
+    copies = [
+        pltpu.make_async_copy(primal_in, primal_ref, sem.at[0]),
+        pltpu.make_async_copy(gradient_in, gradient_ref, sem.at[1]),
+        pltpu.make_async_copy(share_in, share_ref, sem.at[2]),
+    ]
+    for copy in copies:
+        copy.start()
+    for copy in copies:
+        copy.wait()
 
 
 def kernel(
@@ -28,7 +51,6 @@
     share_ref,
     cost_v,
     coef_v,
-    primal_v,
     member_s,
     owner_s,
     local_s,
@@ -43,7 +65,6 @@
     member_in,
     load_sem,
     small_sem,
-    store_sem,
     gather_send,
     gather_recv,
     column_send,
@@ -61,10 +82,10 @@
     barrier = pltpu.get_barrier_semaphore()
 
     def mem_peer(step):
-        return lax.rem(my_mem + step, mem_count)
+        return partner(my_mem, mem_count - step, mem_count)
 
     def job_peer(step):
-        return lax.rem(my_job + step, job_count)
+        return partner(my_job, job_count - step, job_count)
 
     for step in range(1, mem_count):
         pl.semaphore_signal(
@@ -120,7 +141,6 @@
         copy.wait_recv()
 
     lanes = lax.broadcasted_iota(jnp.int32, (block, block), 1)
-    stores = []
     members = jnp.zeros((block, block), jnp.float32)
     for part in range(chunks):
 
@@ -136,7 +156,7 @@
                     coef * dual - cost_v[slot].astype(jnp.float32), 0.0, 1.0
                 )
                 primal = allocation.astype(jnp.bfloat16)
-                primal_v[slot] = primal
+                primal_ref[slot] = primal
                 column[pl.ds(slot, 1), :] = jnp.sum(coef * allocation, axis=0, keepdims=True)
                 halves.append(primal)
                 marks.append((lanes == member_s[0, slot]).astype(jnp.float32).astype(jnp.bfloat16))
@@ -147,10 +167,6 @@
             )
 
         members = lax.fori_loop(0, chunk // 2, pair, members, unroll=2)
-        rows = pl.ds(part * chunk, chunk)
-        copy = pltpu.make_async_copy(primal_v.at[rows], primal_ref.at[rows], store_sem.at[part])
-        copy.start()
-        stores.append(copy)
 
     named = owner_v[...] * jobs + local_v[...]
     match = lax.broadcasted_iota(jnp.int32, (mem_count * jobs, slots), 0) == named
@@ -203,8 +219,6 @@
 
     for copy in gathers + sends + shares:
         copy.wait_send()
-    for copy in stores:
-        copy.wait()
 
 
 def solution(mesh):
@@ -215,23 +229,30 @@
         slots, block, _ = pair_cost.shape
         jobs = duals.shape[0]
         chunks = slots // min(CHUNK, slots)
-        anywhere = pl.BlockSpec(memory_space=pl.ANY)
+        hbm = pl.BlockSpec(memory_space=pltpu.HBM)
+        vmem = pl.BlockSpec(memory_space=pltpu.VMEM)
         dma = pltpu.SemaphoreType.DMA
-        return pl.pallas_call(
+        out_shape = (
+            jax.ShapeDtypeStruct(pair_cost.shape, jnp.bfloat16),
+            jax.ShapeDtypeStruct((jobs, block), jnp.float32),
+            jax.ShapeDtypeStruct((MB_DEV, block), jnp.float32),
+        )
+        operands = (
+            pair_cost,
+            pair_coef,
+            slot_member,
+            slot_owner.reshape(1, slots),
+            slot_local,
+            duals,
+            capacity,
+        )
+        operands = [pltpu.with_memory_space_constraint(value, pltpu.HBM) for value in operands]
+        results = pl.pallas_call(
             functools.partial(kernel, mem_count, job_count),
-            out_shape=(
-                jax.ShapeDtypeStruct(pair_cost.shape, jnp.bfloat16),
-                jax.ShapeDtypeStruct((jobs, block), jnp.float32),
-                jax.ShapeDtypeStruct((MB_DEV, block), jnp.float32),
-            ),
-            in_specs=[anywhere] * 7,
-            out_specs=(
-                anywhere,
-                pl.BlockSpec(memory_space=pltpu.VMEM),
-                pl.BlockSpec(memory_space=pltpu.VMEM),
-            ),
+            out_shape=out_shape,
+            in_specs=[hbm] * 7,
+            out_specs=(vmem,) * 3,
             scratch_shapes=[
-                pltpu.VMEM(pair_cost.shape, jnp.bfloat16),
                 pltpu.VMEM(pair_cost.shape, jnp.bfloat16),
                 pltpu.VMEM(pair_cost.shape, jnp.bfloat16),
                 pltpu.SMEM((1, slots), jnp.int32),
@@ -248,7 +269,6 @@
                 pltpu.VMEM((job_count - 1, MB_DEV, block), jnp.float32),
                 dma((2 * chunks,)),
                 dma((7,)),
-                dma((chunks,)),
                 dma((mem_count - 1,)),
                 dma((mem_count - 1,)),
                 dma((mem_count - 1,)),
@@ -256,16 +276,16 @@
                 dma((job_count - 1,)),
                 dma((job_count - 1,)),
             ],
-            compiler_params=pltpu.CompilerParams(collective_id=0, has_side_effects=True),
-        )(
-            pair_cost,
-            pair_coef,
-            slot_member,
-            slot_owner.reshape(1, slots),
-            slot_local,
-            duals,
-            capacity,
-        )
+            compiler_params=pltpu.CompilerParams(collective_id=0, has_side_effects=True, vmem_limit_bytes=VMEM_LIMIT),
+)(*operands)
+        return pl.pallas_call(
+            finish,
+            out_shape=out_shape,
+            in_specs=[pl.BlockSpec(memory_space=pl.ANY)] * 3,
+            out_specs=(hbm,) * 3,
+            scratch_shapes=[dma((3,))],
+            compiler_params=pltpu.CompilerParams(vmem_limit_bytes=VMEM_LIMIT),
+        )(*results)
 
     return jax.shard_map(
         per_device,

time: 23 us -> 19.1 us (0.83)
  local copies, waits for them, and re-layouts: 3.95 us -> 0 us
    unnamed x7 -> x0, local copies, waits for them, and re-layouts: 3.95 us -> none
    pallas_call x0 -> x1, Pallas kernels: none -> 1.18 us  [per_device(): pl.pallas_call(finish, out_shape=out_shape, in_specs=[pl.BlockSpec(memory...]
    pallas_call x1, Pallas kernels: 18.2 us -> 17.1 us  [per_device(): pl.pallas_call(functools.partial(kernel, mem_count, job_count), out_shape...]
where the time goes in v2:
time: 19.1 us; the launch traced here: 19 us
  Pallas kernels  18.3 us (96%)
  between operations  0.64 us (3%)
    pallas_call x1, Pallas kernels, per_device(): pl.pallas_call(functools.partial(kernel, mem_count, job_count), out_shape...  17.1 us
    pallas_call x1, Pallas kernels, per_device(): pl.pallas_call(finish, out_shape=out_shape, in_specs=[pl.BlockSpec(memory...  1.18 us

profile of v2, /device:TPU:0, one launch (start us, length us, event | category | flops | bytes accessed | tf_op | source)
XLA Modules:
  0.0 19.0 jit_solution(16412364822458951177)
XLA Ops:
  0.6 17.1 %shard_map.94 = (bf16[48,128,128]{2,1,0:T(8,128)(2,1)S(1)}, f32[16,128]{1,0:T(8,128)S(1)}, f32[32,128]{1,0:T(8,128)S(1)}) custom-call(bf16[48,128,128]{2,1,0:T(8,128)(2,1)} %cost_ref.1, bf16[48,128,128]{2,1,0:T(8,128)(2,1)} %coef_ref.1, s32[1,48]{1,0:T(1,128)} %member_ref.1, s32[1,48]{1,0:T(1,128)} %bitcast.1, s32[1,48]{1,0:T(1,128)} %local_ref.1, ...), custom_call_target="tpu_custom_call" | custom-call | tf_op jit(solution)/shard_map/pallas_call | solution.py:250
  17.8 1.2 %shard_map.95 = (bf16[48,128,128]{2,1,0:T(8,128)(2,1)}, f32[16,128]{1,0:T(8,128)}, f32[32,128]{1,0:T(8,128)}) custom-call(bf16[48,128,128]{2,1,0:T(8,128)(2,1)S(1)} %get-tuple-element.6.primal_in, f32[16,128]{1,0:T(8,128)S(1)} %get-tuple-element.7.gradient_in, f32[32,128]{1,0:T(8,128)S(1)} %get-tuple-element.8.share_in), custom_call_target="tpu_custom_call" | custom-call | tf_op jit(solution)/shard_map/pallas_call | solution.py:281

commit v3 on v2

--- a/solution.py
+++ b/solution.py
@@ -9,6 +9,7 @@
 
 MB_DEV = 32
 CHUNK = 8
+LEVELS = 4
 VMEM_LIMIT = 16 << 20
 
 MESH = pl.DeviceIdType.MESH
@@ -39,6 +40,7 @@
 def kernel(
     mem_count,
     job_count,
+    low,
     cost_ref,
     coef_ref,
     member_ref,
@@ -65,8 +67,12 @@
     member_in,
     load_sem,
     small_sem,
-    gather_send,
-    gather_recv,
+    beside_send,
+    beside_recv,
+    down_send,
+    down_recv,
+    up_send,
+    up_recv,
     column_send,
     column_recv,
     member_send,
@@ -78,6 +84,9 @@
     chunks = slots // chunk
     my_mem = lax.axis_index("mem")
     my_job = lax.axis_index("job")
+    levels = mem_count // low
+    level = my_mem // low
+    place = my_mem % low
 
     barrier = pltpu.get_barrier_semaphore()
 
@@ -87,10 +96,23 @@
     def job_peer(step):
         return partner(my_job, job_count - step, job_count)
 
-    for step in range(1, mem_count):
-        pl.semaphore_signal(
-            barrier, inc=1, device_id=(mem_peer(step), my_job), device_id_type=MESH
-        )
+    def announce(mem):
+        pl.semaphore_signal(barrier, inc=1, device_id=(mem, my_job), device_id_type=MESH)
+
+    for distance in reversed(range(1, levels)):
+
+        @pl.when(level + distance < levels)
+        def _(distance=distance):
+            for shift in range(low):
+                announce((level + distance) * low + partner(place, shift, low))
+
+    for shift in range(1, low):
+        announce(level * low + partner(place, shift, low))
+
+    @pl.when(level > 0)
+    def _():
+        announce(my_mem - low)
+
     for step in range(1, job_count):
         pl.semaphore_signal(
             barrier, inc=1, device_id=(my_mem, job_peer(step)), device_id_type=MESH
@@ -119,26 +141,84 @@
             loads.append(copy)
     small[0].wait()
 
-    pl.semaphore_wait(barrier, mem_count + job_count - 2)
-
-    gathers = []
-    for step in range(1, mem_count):
-        copy = pltpu.make_async_remote_copy(
-            src_ref=table.at[own_rows],
-            dst_ref=table.at[own_rows],
-            send_sem=gather_send.at[step - 1],
-            recv_sem=gather_recv.at[step - 1],
-            device_id=(mem_peer(step), my_job),
+    above = jnp.where(level < levels - 1, 1, 0)
+    pl.semaphore_wait(barrier, job_count - 1 + low - 1 + level * low + above)
+
+    def push(rows, mem, send_sem, recv_sem):
+        return pltpu.make_async_remote_copy(
+            src_ref=table.at[rows],
+            dst_ref=table.at[rows],
+            send_sem=send_sem,
+            recv_sem=recv_sem,
+            device_id=(mem, my_job),
             device_id_type=MESH,
         )
-        copy.start()
-        gathers.append(copy)
+
+    def beside(shift):
+        mem = level * low + partner(place, shift, low)
+        return push(own_rows, mem, beside_send.at[shift - 1], beside_recv.at[shift - 1])
+
+    def down(distance, shift):
+        mem = (level - distance) * low + partner(place, shift, low)
+        index = (distance - 1) * low + shift
+        return push(own_rows, mem, down_send.at[index], down_recv.at[index])
+
+    def up(origin, shift):
+        first = (origin * low + partner(place, shift, low)) * jobs
+        rows = pl.ds(pl.multiple_of(first, jobs), jobs)
+        index = origin * low + shift
+        return push(rows, my_mem + low, up_send.at[index], up_recv.at[index])
+
+    @pl.when(level < levels - 1)
+    def _():
+        for origin in range(levels - 1):
+
+            @pl.when(level == origin)
+            def _(origin=origin):
+                up(origin, 0).start()
+
+    for shift in range(1, low):
+        beside(shift).start()
+    for distance in reversed(range(1, levels)):
+
+        @pl.when(level >= distance)
+        def _(distance=distance):
+            for shift in range(low):
+                down(distance, shift).start()
+
+    for origin in range(levels - 1):
+        for shift in range(low):
+
+            @pl.when(level > origin)
+            def _(origin=origin, shift=shift):
+                up(origin, shift).wait_recv()
+
+            @pl.when((level > origin) & (level < levels - 1))
+            def _(origin=origin, shift=shift):
+                up(origin, shift).start()
+
+        @pl.when(level == origin)
+        def _(origin=origin):
+            for shift in range(1, low):
+                beside(shift).wait_recv()
+                up(origin, shift).start()
+
+    @pl.when(level == levels - 1)
+    def _():
+        for shift in range(1, low):
+            beside(shift).wait_recv()
+
     for copy in small[1:]:
         copy.wait()
     for copy in loads:
         copy.wait()
-    for copy in gathers:
-        copy.wait_recv()
+    for distance in range(1, levels):
+
+        @pl.when(level + distance < levels)
+        def _(distance=distance):
+            for shift in range(low):
+                down(distance, shift).wait_recv()
+
 
     lanes = lax.broadcasted_iota(jnp.int32, (block, block), 1)
     members = jnp.zeros((block, block), jnp.float32)
@@ -173,9 +253,9 @@
     match = match.astype(jnp.float32).astype(jnp.bfloat16)
     sums = column[...]
     high = sums.astype(jnp.bfloat16)
-    low = (sums - high.astype(jnp.float32)).astype(jnp.bfloat16)
+    rest = (sums - high.astype(jnp.float32)).astype(jnp.bfloat16)
     totals[...] = jnp.dot(match, high, preferred_element_type=jnp.float32) + jnp.dot(
-        match, low, preferred_element_type=jnp.float32
+        match, rest, preferred_element_type=jnp.float32
     )
     member_part[...] = members.T[:MB_DEV]
 
@@ -217,12 +297,28 @@
         gradient = gradient + incoming[step]
     gradient_ref[...] = gradient
 
-    for copy in gathers + sends + shares:
+    for copy in sends + shares:
         copy.wait_send()
+    for shift in range(1, low):
+        beside(shift).wait_send()
+    for distance in range(1, levels):
+
+        @pl.when(level >= distance)
+        def _(distance=distance):
+            for shift in range(low):
+                down(distance, shift).wait_send()
+
+    for origin in range(levels - 1):
+
+        @pl.when((level >= origin) & (level < levels - 1))
+        def _(origin=origin):
+            for shift in range(low):
+                up(origin, shift).wait_send()
 
 
 def solution(mesh):
     mem_count, job_count = mesh.shape["mem"], mesh.shape["job"]
+    low = 2 if mem_count <= LEVELS * 2 else mem_count
     row = P(("mem", "job"))
 
     def per_device(pair_cost, pair_coef, slot_member, slot_owner, slot_local, duals, capacity):
@@ -248,7 +344,7 @@
         )
         operands = [pltpu.with_memory_space_constraint(value, pltpu.HBM) for value in operands]
         results = pl.pallas_call(
-            functools.partial(kernel, mem_count, job_count),
+            functools.partial(kernel, mem_count, job_count, low),
             out_shape=out_shape,
             in_specs=[hbm] * 7,
             out_specs=(vmem,) * 3,
@@ -269,8 +365,12 @@
                 pltpu.VMEM((job_count - 1, MB_DEV, block), jnp.float32),
                 dma((2 * chunks,)),
                 dma((7,)),
-                dma((mem_count - 1,)),
-                dma((mem_count - 1,)),
+                dma((max(low - 1, 1),)),
+                dma((max(low - 1, 1),)),
+                dma((mem_count,)),
+                dma((mem_count,)),
+                dma((mem_count,)),
+                dma((mem_count,)),
                 dma((mem_count - 1,)),
                 dma((mem_count - 1,)),
                 dma((job_count - 1,)),

time: 19.1 us -> 23.3 us (1.22)
  Pallas kernels: 18.3 us -> 22.5 us
    pallas_call x1, Pallas kernels: 17.1 us -> 21.4 us  [per_device(): pl.pallas_call(functools.partial(kernel, mem_count, job_count, low), out_...]
where the time goes in v3:
time: 23.3 us; the launch traced here: 23.2 us
  Pallas kernels  22.5 us (97%)
  between operations  0.64 us (3%)
    pallas_call x1, Pallas kernels, per_device(): pl.pallas_call(functools.partial(kernel, mem_count, job_count, low), out_...  21.4 us
    pallas_call x1, Pallas kernels, per_device(): pl.pallas_call(finish, out_shape=out_shape, in_specs=[pl.BlockSpec(memory...  1.18 us

profile of v3, /device:TPU:0, one launch (start us, length us, event | category | flops | bytes accessed | tf_op | source)
XLA Modules:
  0.0 23.2 jit_solution(12278556811627884356)
XLA Ops:
  0.6 21.4 %shard_map.94 = (bf16[48,128,128]{2,1,0:T(8,128)(2,1)S(1)}, f32[16,128]{1,0:T(8,128)S(1)}, f32[32,128]{1,0:T(8,128)S(1)}) custom-call(bf16[48,128,128]{2,1,0:T(8,128)(2,1)} %cost_ref.1, bf16[48,128,128]{2,1,0:T(8,128)(2,1)} %coef_ref.1, s32[1,48]{1,0:T(1,128)} %member_ref.1, s32[1,48]{1,0:T(1,128)} %bitcast.1, s32[1,48]{1,0:T(1,128)} %local_ref.1, ...), custom_call_target="tpu_custom_call" | custom-call | tf_op jit(solution)/shard_map/pallas_call | solution.py:346
  22.0 1.2 %shard_map.95 = (bf16[48,128,128]{2,1,0:T(8,128)(2,1)}, f32[16,128]{1,0:T(8,128)}, f32[32,128]{1,0:T(8,128)}) custom-call(bf16[48,128,128]{2,1,0:T(8,128)(2,1)S(1)} %get-tuple-element.6.primal_in, f32[16,128]{1,0:T(8,128)S(1)} %get-tuple-element.7.gradient_in, f32[32,128]{1,0:T(8,128)S(1)} %get-tuple-element.8.share_in), custom_call_target="tpu_custom_call" | custom-call | tf_op jit(solution)/shard_map/pallas_call | solution.py:381

commit v4 on v2

--- a/solution.py
+++ b/solution.py
@@ -9,6 +9,7 @@
 
 MB_DEV = 32
 CHUNK = 8
+GROUP = 8
 VMEM_LIMIT = 16 << 20
 
 MESH = pl.DeviceIdType.MESH
@@ -26,10 +27,16 @@
 
 def finish(primal_in, gradient_in, share_in, primal_ref, gradient_ref, share_ref, sem):
     copies = [
-        pltpu.make_async_copy(primal_in, primal_ref, sem.at[0]),
-        pltpu.make_async_copy(gradient_in, gradient_ref, sem.at[1]),
-        pltpu.make_async_copy(share_in, share_ref, sem.at[2]),
+        pltpu.make_async_copy(gradient_in, gradient_ref, sem.at[0]),
+        pltpu.make_async_copy(share_in, share_ref, sem.at[1]),
     ]
+    slots = primal_in.shape[0]
+    chunk = min(CHUNK, slots)
+    for part in range(slots // chunk):
+        rows = pl.ds(part * chunk, chunk)
+        copies.append(
+            pltpu.make_async_copy(primal_in.at[rows], primal_ref.at[rows], sem.at[2 + part])
+        )
     for copy in copies:
         copy.start()
     for copy in copies:
@@ -142,31 +149,27 @@
 
     lanes = lax.broadcasted_iota(jnp.int32, (block, block), 1)
     members = jnp.zeros((block, block), jnp.float32)
-    for part in range(chunks):
-
-        def pair(index, members, part=part):
-            halves = []
-            marks = []
-            for side in range(2):
-                slot = part * chunk + 2 * index + side
-                row = owner_s[0, slot] * jobs + local_s[0, slot]
-                dual = -table[pl.ds(row, 1), :]
-                coef = coef_v[slot].astype(jnp.float32)
-                allocation = jnp.clip(
-                    coef * dual - cost_v[slot].astype(jnp.float32), 0.0, 1.0
-                )
-                primal = allocation.astype(jnp.bfloat16)
-                primal_ref[slot] = primal
-                column[pl.ds(slot, 1), :] = jnp.sum(coef * allocation, axis=0, keepdims=True)
-                halves.append(primal)
-                marks.append((lanes == member_s[0, slot]).astype(jnp.float32).astype(jnp.bfloat16))
-            return members + jnp.dot(
-                jnp.concatenate(halves, axis=1),
-                jnp.concatenate(marks, axis=0),
-                preferred_element_type=jnp.float32,
-            )
-
-        members = lax.fori_loop(0, chunk // 2, pair, members, unroll=2)
+    def group(index, members):
+        parts = []
+        marks = []
+        for side in range(GROUP):
+            slot = GROUP * index + side
+            row = owner_s[0, slot] * jobs + local_s[0, slot]
+            dual = -table[pl.ds(row, 1), :]
+            coef = coef_v[slot].astype(jnp.float32)
+            allocation = jnp.clip(coef * dual - cost_v[slot].astype(jnp.float32), 0.0, 1.0)
+            primal = allocation.astype(jnp.bfloat16)
+            primal_ref[slot] = primal
+            column[pl.ds(slot, 1), :] = jnp.sum(coef * allocation, axis=0, keepdims=True)
+            parts.append(primal)
+            marks.append((lanes == member_s[0, slot]).astype(jnp.float32).astype(jnp.bfloat16))
+        return members + jnp.dot(
+            jnp.concatenate(parts, axis=1),
+            jnp.concatenate(marks, axis=0),
+            preferred_element_type=jnp.float32,
+        )
+
+    members = lax.fori_loop(0, slots // GROUP, group, members)
 
     named = owner_v[...] * jobs + local_v[...]
     match = lax.broadcasted_iota(jnp.int32, (mem_count * jobs, slots), 0) == named
@@ -276,14 +279,16 @@
                 dma((job_count - 1,)),
                 dma((job_count - 1,)),
             ],
-            compiler_params=pltpu.CompilerParams(collective_id=0, has_side_effects=True, vmem_limit_bytes=VMEM_LIMIT),
-)(*operands)
+            compiler_params=pltpu.CompilerParams(
+                collective_id=0, has_side_effects=True, vmem_limit_bytes=VMEM_LIMIT
+            ),
+        )(*operands)
         return pl.pallas_call(
             finish,
             out_shape=out_shape,
             in_specs=[pl.BlockSpec(memory_space=pl.ANY)] * 3,
             out_specs=(hbm,) * 3,
-            scratch_shapes=[dma((3,))],
+            scratch_shapes=[dma((2 + chunks,))],
             compiler_params=pltpu.CompilerParams(vmem_limit_bytes=VMEM_LIMIT),
         )(*results)
 

time: 19.1 us -> 18.3 us (0.958)
  Pallas kernels: 18.3 us -> 17.6 us
    pallas_call x1, Pallas kernels: 17.1 us -> 16.3 us  [per_device(): pl.pallas_call(functools.partial(kernel, mem_count, job_count), out_shape...]
where the time goes in v4:
time: 18.3 us; the launch traced here: 18.2 us
  Pallas kernels  17.6 us (96%)
  between operations  0.64 us (3%)
    pallas_call x1, Pallas kernels, per_device(): pl.pallas_call(functools.partial(kernel, mem_count, job_count), out_shape...  16.3 us
    pallas_call x1, Pallas kernels, per_device(): pl.pallas_call(finish, out_shape=out_shape, in_specs=[pl.BlockSpec(memory...  1.21 us

profile of v4, /device:TPU:0, one launch (start us, length us, event | category | flops | bytes accessed | tf_op | source)
XLA Modules:
  0.0 18.2 jit_solution(1428745504949215099)
XLA Ops:
  0.6 16.3 %shard_map.94 = (bf16[48,128,128]{2,1,0:T(8,128)(2,1)S(1)}, f32[16,128]{1,0:T(8,128)S(1)}, f32[32,128]{1,0:T(8,128)S(1)}) custom-call(bf16[48,128,128]{2,1,0:T(8,128)(2,1)} %cost_ref.1, bf16[48,128,128]{2,1,0:T(8,128)(2,1)} %coef_ref.1, s32[1,48]{1,0:T(1,128)} %member_ref.1, s32[1,48]{1,0:T(1,128)} %bitcast.1, s32[1,48]{1,0:T(1,128)} %local_ref.1, ...), custom_call_target="tpu_custom_call" | custom-call | tf_op jit(solution)/shard_map/pallas_call | solution.py:253
  17.0 1.2 %shard_map.95 = (bf16[48,128,128]{2,1,0:T(8,128)(2,1)}, f32[16,128]{1,0:T(8,128)}, f32[32,128]{1,0:T(8,128)}) custom-call(bf16[48,128,128]{2,1,0:T(8,128)(2,1)S(1)} %get-tuple-element.6.primal_in, f32[16,128]{1,0:T(8,128)S(1)} %get-tuple-element.7.gradient_in, f32[32,128]{1,0:T(8,128)S(1)} %get-tuple-element.8.share_in), custom_call_target="tpu_custom_call" | custom-call | tf_op jit(solution)/shard_map/pallas_call | solution.py:286

commit v5 on v4

--- a/solution.py
+++ b/solution.py
@@ -147,29 +147,18 @@
     for copy in gathers:
         copy.wait_recv()
 
-    lanes = lax.broadcasted_iota(jnp.int32, (block, block), 1)
-    members = jnp.zeros((block, block), jnp.float32)
-    def group(index, members):
-        parts = []
-        marks = []
+    def allocate(index, carry):
         for side in range(GROUP):
             slot = GROUP * index + side
             row = owner_s[0, slot] * jobs + local_s[0, slot]
             dual = -table[pl.ds(row, 1), :]
             coef = coef_v[slot].astype(jnp.float32)
             allocation = jnp.clip(coef * dual - cost_v[slot].astype(jnp.float32), 0.0, 1.0)
-            primal = allocation.astype(jnp.bfloat16)
-            primal_ref[slot] = primal
+            primal_ref[slot] = allocation.astype(jnp.bfloat16)
             column[pl.ds(slot, 1), :] = jnp.sum(coef * allocation, axis=0, keepdims=True)
-            parts.append(primal)
-            marks.append((lanes == member_s[0, slot]).astype(jnp.float32).astype(jnp.bfloat16))
-        return members + jnp.dot(
-            jnp.concatenate(parts, axis=1),
-            jnp.concatenate(marks, axis=0),
-            preferred_element_type=jnp.float32,
-        )
-
-    members = lax.fori_loop(0, slots // GROUP, group, members)
+        return carry
+
+    lax.fori_loop(0, slots // GROUP, allocate, 0)
 
     named = owner_v[...] * jobs + local_v[...]
     match = lax.broadcasted_iota(jnp.int32, (mem_count * jobs, slots), 0) == named
@@ -180,7 +169,6 @@
     totals[...] = jnp.dot(match, high, preferred_element_type=jnp.float32) + jnp.dot(
         match, low, preferred_element_type=jnp.float32
     )
-    member_part[...] = members.T[:MB_DEV]
 
     sends = []
     for step in range(1, mem_count):
@@ -195,6 +183,25 @@
         )
         copy.start()
         sends.append(copy)
+    lanes = lax.broadcasted_iota(jnp.int32, (block, block), 1)
+
+    def group(index, members):
+        first = GROUP * index
+        parts = [primal_ref[first + side] for side in range(GROUP)]
+        marks = [
+            (lanes == member_s[0, first + side]).astype(jnp.float32).astype(jnp.bfloat16)
+            for side in range(GROUP)
+        ]
+        return members + jnp.dot(
+            jnp.concatenate(parts, axis=1),
+            jnp.concatenate(marks, axis=0),
+            preferred_element_type=jnp.float32,
+        )
+
+    members = lax.fori_loop(
+        0, slots // GROUP, group, jnp.zeros((block, block), jnp.float32)
+    )
+    member_part[...] = members.T[:MB_DEV]
     shares = []
     for step in range(1, job_count):
         copy = pltpu.make_async_remote_copy(

time: 18.3 us -> 17.6 us (0.962)
  Pallas kernels: 17.6 us -> 16.8 us
    pallas_call x1, Pallas kernels: 16.3 us -> 15.6 us  [per_device(): pl.pallas_call(functools.partial(kernel, mem_count, job_count), out_shape...]
where the time goes in v5:
time: 17.6 us; the launch traced here: 17.4 us
  Pallas kernels  16.8 us (95%)
  between operations  0.64 us (4%)
    pallas_call x1, Pallas kernels, per_device(): pl.pallas_call(functools.partial(kernel, mem_count, job_count), out_shape...  15.6 us
    pallas_call x1, Pallas kernels, per_device(): pl.pallas_call(finish, out_shape=out_shape, in_specs=[pl.BlockSpec(memory...  1.21 us

profile of v5, /device:TPU:0, one launch (start us, length us, event | category | flops | bytes accessed | tf_op | source)
XLA Modules:
  0.0 17.4 jit_solution(13163222440446678192)
XLA Ops:
  0.6 15.6 %shard_map.94 = (bf16[48,128,128]{2,1,0:T(8,128)(2,1)S(1)}, f32[16,128]{1,0:T(8,128)S(1)}, f32[32,128]{1,0:T(8,128)S(1)}) custom-call(bf16[48,128,128]{2,1,0:T(8,128)(2,1)} %cost_ref.1, bf16[48,128,128]{2,1,0:T(8,128)(2,1)} %coef_ref.1, s32[1,48]{1,0:T(1,128)} %member_ref.1, s32[1,48]{1,0:T(1,128)} %bitcast.1, s32[1,48]{1,0:T(1,128)} %local_ref.1, ...), custom_call_target="tpu_custom_call" | custom-call | tf_op jit(solution)/shard_map/pallas_call | solution.py:260
  16.2 1.2 %shard_map.95 = (bf16[48,128,128]{2,1,0:T(8,128)(2,1)}, f32[16,128]{1,0:T(8,128)}, f32[32,128]{1,0:T(8,128)}) custom-call(bf16[48,128,128]{2,1,0:T(8,128)(2,1)S(1)} %get-tuple-element.6.primal_in, f32[16,128]{1,0:T(8,128)S(1)} %get-tuple-element.7.gradient_in, f32[32,128]{1,0:T(8,128)S(1)} %get-tuple-element.8.share_in), custom_call_target="tpu_custom_call" | custom-call | tf_op jit(solution)/shard_map/pallas_call | solution.py:293

commit v6 on v5

--- a/solution.py
+++ b/solution.py
@@ -128,18 +128,26 @@
 
     pl.semaphore_wait(barrier, mem_count + job_count - 2)
 
-    gathers = []
-    for step in range(1, mem_count):
-        copy = pltpu.make_async_remote_copy(
+    def gather(peer, index):
+        return pltpu.make_async_remote_copy(
             src_ref=table.at[own_rows],
             dst_ref=table.at[own_rows],
-            send_sem=gather_send.at[step - 1],
-            recv_sem=gather_recv.at[step - 1],
-            device_id=(mem_peer(step), my_job),
+            send_sem=gather_send.at[index],
+            recv_sem=gather_recv.at[index],
+            device_id=(peer, my_job),
             device_id_type=MESH,
         )
-        copy.start()
-        gathers.append(copy)
+
+    def index_of(target):
+        return mem_count - 1 - partner(my_mem, target, mem_count)
+
+    gathers = [gather(mem_peer(step), step - 1) for step in range(1, mem_count)]
+    for target in reversed(range(mem_count)):
+
+        @pl.when(my_mem != target)
+        def _(target=target):
+            gather(target, index_of(target)).start()
+
     for copy in small[1:]:
         copy.wait()
     for copy in loads:
@@ -170,19 +178,23 @@
         match, low, preferred_element_type=jnp.float32
     )
 
-    sends = []
-    for step in range(1, mem_count):
-        peer = mem_peer(step)
-        copy = pltpu.make_async_remote_copy(
+    def send(peer, index):
+        return pltpu.make_async_remote_copy(
             src_ref=totals.at[pl.ds(pl.multiple_of(peer * jobs, jobs), jobs)],
-            dst_ref=incoming.at[step - 1],
-            send_sem=column_send.at[step - 1],
-            recv_sem=column_recv.at[step - 1],
+            dst_ref=incoming.at[index],
+            send_sem=column_send.at[index],
+            recv_sem=column_recv.at[index],
             device_id=(peer, my_job),
             device_id_type=MESH,
         )
-        copy.start()
-        sends.append(copy)
+
+    sends = [send(mem_peer(step), step - 1) for step in range(1, mem_count)]
+    for target in range(mem_count):
+
+        @pl.when(my_mem != target)
+        def _(target=target):
+            send(target, index_of(target)).start()
+
     lanes = lax.broadcasted_iota(jnp.int32, (block, block), 1)
 
     def group(index, members):

time: 17.6 us -> 17.7 us (level)
  no operation moved by 1% of the time
where the time goes in v6:
time: 17.7 us; the launch traced here: 17.5 us
  Pallas kernels  16.9 us (95%)
  between operations  0.64 us (4%)
    pallas_call x1, Pallas kernels, per_device(): pl.pallas_call(functools.partial(kernel, mem_count, job_count), out_shape...  15.7 us
    pallas_call x1, Pallas kernels, per_device(): pl.pallas_call(finish, out_shape=out_shape, in_specs=[pl.BlockSpec(memory...  1.21 us

profile of v6, /device:TPU:0, one launch (start us, length us, event | category | flops | bytes accessed | tf_op | source)
XLA Modules:
  0.0 17.5 jit_solution(3237966036711652148)
XLA Ops:
  0.6 15.7 %shard_map.94 = (bf16[48,128,128]{2,1,0:T(8,128)(2,1)S(1)}, f32[16,128]{1,0:T(8,128)S(1)}, f32[32,128]{1,0:T(8,128)S(1)}) custom-call(bf16[48,128,128]{2,1,0:T(8,128)(2,1)} %cost_ref.1, bf16[48,128,128]{2,1,0:T(8,128)(2,1)} %coef_ref.1, s32[1,48]{1,0:T(1,128)} %member_ref.1, s32[1,48]{1,0:T(1,128)} %bitcast.1, s32[1,48]{1,0:T(1,128)} %local_ref.1, ...), custom_call_target="tpu_custom_call" | custom-call | tf_op jit(solution)/shard_map/pallas_call | solution.py:272
  16.3 1.2 %shard_map.95 = (bf16[48,128,128]{2,1,0:T(8,128)(2,1)}, f32[16,128]{1,0:T(8,128)}, f32[32,128]{1,0:T(8,128)}) custom-call(bf16[48,128,128]{2,1,0:T(8,128)(2,1)S(1)} %get-tuple-element.6.primal_in, f32[16,128]{1,0:T(8,128)S(1)} %get-tuple-element.7.gradient_in, f32[32,128]{1,0:T(8,128)S(1)} %get-tuple-element.8.share_in), custom_call_target="tpu_custom_call" | custom-call | tf_op jit(solution)/shard_map/pallas_call | solution.py:305
